TPU v7x, 32 devices: a whole 2x2x4 slice. The times are simulated.
32 devices in a mesh: hid: 4 (over y, x), tok: 8 (over z, core).
Axes of the slice: x: 2, y: 2, z: 4, core: 2. Of those that a mesh axis runs over, the one named last changes fastest.
Arguments:
- keys: bfloat16 [2, 512, 1280], P(None, 'tok'), may hold values from -6 to 6
- values: bfloat16 [2, 512, 1280], P(None, 'tok'), may hold values from -6 to 6
- queries: bfloat16 [512, 1280], P('tok'), may hold values from -6 to 6
- rates: float32 [2, 512], P(None, 'tok'), may hold values from 0.01 to 0.1
- forget: float32 [2], replicated, may hold values from 0.05 to 0.3
- momentum: float32 [1], replicated, may hold values from 0.5 to 0.95
- write_weight: float32 [1280, 1280], P('tok', 'hid'), may hold values from -0.15625 to 0.15625
- read_weight: float32 [1280, 1280], P('tok', 'hid'), may hold values from -0.15625 to 0.15625
Outputs:
- new_write: float32 [1280, 1280], P('tok', 'hid')
- new_read: float32 [1280, 1280], P('tok', 'hid')
- recalled: bfloat16 [512, 1280], P('tok')
All inputs are finite; a program needn't handle non-finite values.
Results may differ from a plain program's by a relative error of at most 0.003.
Values may be sent and summed in bfloat16 or wider, within the bound.
No kernel may reach another device: no remote copies, remote signals or barrier semaphores. Data moves between devices by JAX's collectives and lax.ppermute only.
A program may use at most 64 MiB of HBM per device.

v0:
```python
import jax
import jax.numpy as jnp
from jax import lax
from jax.sharding import PartitionSpec as P

highest = lax.Precision.HIGHEST
radius = 12.0


def silu_slope(z):
    sig = jax.nn.sigmoid(z)
    return sig * (1.0 + z * (1.0 - sig))


def times_transposed(left, right):
    return lax.dot_general(left, right, (((1,), (1,)), ((), ())), precision=highest)


def inner_rows(left, right):
    return lax.dot_general(left, right, (((0,), (0,)), ((), ())), precision=highest)


def on_device(keys, values, queries, rates, forget, momentum, write_weight, read_weight):
    width = keys.shape[2]
    full_write, full_read = (
        lax.all_gather(write_weight, "tok", axis=0, tiled=True),
        lax.all_gather(read_weight, "tok", axis=0, tiled=True),
    )
    inputs = keys.reshape(-1, width).astype(jnp.float32)
    hidden_pre = jnp.dot(inputs, full_write, precision=highest)
    hidden = jax.nn.silu(hidden_pre)
    output = lax.psum(times_transposed(hidden, full_read).astype(jnp.bfloat16), "hid").astype(
        jnp.float32
    )
    error = inputs + output - values.reshape(-1, width).astype(jnp.float32)
    factor = 1.0 - forget[1] + momentum[0]
    per_block = jnp.stack([factor, jnp.ones_like(factor)])
    row_scale = (2.0 * rates * per_block[:, None]).reshape(-1, 1)
    delta = row_scale * error
    back = jnp.dot(delta, full_read, precision=highest) * silu_slope(hidden_pre)
    grad_write = inner_rows(inputs, back)
    grad_read = inner_rows(delta, hidden)
    part_w, part_r = (
        lax.psum_scatter(grad_write, "tok", scatter_dimension=0, tiled=True),
        lax.psum_scatter(grad_read, "tok", scatter_dimension=0, tiled=True),
    )
    keep = (1.0 - forget[0]) * (1.0 - forget[1])
    whole_w, whole_r = (
        lax.all_gather(part_w, "tok", axis=0, tiled=True),
        lax.all_gather(part_r, "tok", axis=0, tiled=True),
    )
    total = lax.psum(jnp.sum(whole_w * whole_w) + jnp.sum(whole_r * whole_r), "hid")
    scale = jnp.minimum(1.0, radius / jnp.sqrt(total + 1e-06))
    new_write = keep * write_weight - scale * part_w
    new_read = keep * read_weight - scale * part_r
    wide_write = keep * full_write - scale * whole_w
    wide_read = keep * full_read - scale * whole_r
    asked = queries.astype(jnp.float32)
    query_hidden = jax.nn.silu(jnp.dot(asked, wide_write, precision=highest))
    answer = lax.psum(times_transposed(query_hidden, wide_read), "hid")
    recalled = (asked + answer).astype(jnp.bfloat16)
    return (new_write, new_read, recalled)


def solution(mesh):
    in_specs = (
        P(None, "tok", None),
        P(None, "tok", None),
        P("tok", None),
        P(None, "tok"),
        P(),
        P(),
        P("tok", "hid"),
        P("tok", "hid"),
    )
    out_specs = (P("tok", "hid"), P("tok", "hid"), P("tok", None))
    return jax.shard_map(
        on_device, mesh=mesh, in_specs=in_specs, out_specs=out_specs, check_vma=False
    )
```

profile of v0, /device:TPU:0, one launch (start us, length us, event | category | flops | bytes accessed | tf_op | source)
XLA Modules:
  0.0 327.0 jit_solution(6038212173051882562)
XLA Ops:
  7.2 0.0 all-gather.5.cloned.1.call-start
  7.2 0.7 all-gather.5.cloned.1.call-update
  7.9 0.0 all-gather.7.cloned.1.call-start
  7.9 0.7 all-gather.7.cloned.1.call-update
  8.6 0.0 all-reduce.3.cloned.1.call-start
  9.3 1.3 fusion.33
  11.3 29.1 %all-gather.5.cloned.1.call-done = f32[1280,320]{1,0:T(8,128)} async-done(((f32[160,320]{1,0:T(8,128)}), f32[1280,320]{1,0:T(8,128)}) %all-gather.5.cloned.1.call-update) | async-done | bytes 1638416 | tf_op jit(solution)/shard_map/all_gather | solution.py:26
  40.4 3.4 %fusion.34 = f32[128,320]{0,1:T(8,128)S(1)} fusion(bf16[128,1280]{1,0:T(8,128)(2,1)} %bitcast.17, f32[1280,320]{1,0:T(8,128)} %all-gather.5.cloned.1.call-done), kind=kOutput, calls=%fused_computation.40 | convolution fusion | flops 629145600 | bytes 2129920 | tf_op jit(solution)/shard_map/dot_general | solution.py:30
  43.8 0.0 copy-start.10
  43.8 0.0 copy-start.2
  43.8 0.0 copy-start.3
  43.8 25.7 %all-gather.7.cloned.1.call-done = f32[1280,320]{1,0:T(8,128)} async-done(((f32[160,320]{1,0:T(8,128)}), f32[1280,320]{1,0:T(8,128)}) %all-gather.7.cloned.1.call-update) | async-done | bytes 1638416 | tf_op jit(solution)/shard_map/all_gather | solution.py:27
  69.6 4.6 %convolution_convert_fusion = bf16[128,1280]{1,0:T(8,128)(2,1)} fusion(f32[1280,320]{1,0:T(8,128)} %all-gather.7.cloned.1.call-done, f32[128,320]{0,1:T(8,128)S(1)} %fusion.34), kind=kOutput, calls=%fused_computation.1 | convolution fusion | flops 629473280 | bytes 2129920 | tf_op jit(solution)/shard_map/dot_general | solution.py:16
  74.2 0.0 all-reduce.3.cloned.1.call-update
  74.2 0.0 reduce-scatter.7.cloned.1.call-start
  74.3 0.1 maximum_multiply_fusion
  74.3 0.0 copy-done.10
  74.3 0.1 broadcast_multiply_fusion
  74.4 0.1 mul.101
  74.5 42.8 %all-reduce.3.cloned.1.call-done = bf16[128,1280]{1,0:T(8,128)(2,1)} async-done(((bf16[128,1280]{1,0:T(8,128)(2,1)}), bf16[128,1280]{1,0:T(8,128)(2,1)}) %all-reduce.3.cloned.1.call-update) | async-done | bytes 327696 | tf_op jit(solution)/shard_map/psum | solution.py:32
  117.3 0.0 copy-done.2
  117.4 0.0 copy-done.3
  117.4 0.0 copy-done
  117.4 4.3 %convolution_multiply_fusion = f32[128,320]{0,1:T(8,128)S(1)} fusion(f32[1280,320]{1,0:T(8,128)S(1)} %copy-done, bf16[128,1280]{1,0:T(8,128)(2,1)S(1)} %bitcast.21, bf16[128,1280]{1,0:T(8,128)(2,1)} %all-reduce.3.cloned.1.call-done, bf16[128,1280]{1,0:T(8,128)(2,1)S(1)} %bitcast.18, f32[128]{0:T(128)S(1)} %mul.101, f32[128,320]{0,1:T(8,128)S(1)} %fusion.34), kind=kOutput, calls=%fused_computation.12 | convolution fusion | flops 630456320 | bytes 2949632 | tf_op jit(solution)/shard_map/dot_general | solution.py:40
  121.6 2.0 convolution_bitcast_fusion
  123.6 2.8 copy.26
  126.4 0.0 reduce-scatter.7.cloned.1.call-update
  126.5 0.0 reduce-scatter.9.cloned.1.call-start
  126.5 0.0 copy-done.4
  126.5 3.7 %fusion.16 = f32[1280,320]{1,0:T(8,128)} fusion(bf16[128,1280]{1,0:T(8,128)(2,1)S(1)} %bitcast.22, bf16[128,1280]{1,0:T(8,128)(2,1)S(1)} %copy-done.4, bf16[128,1280]{1,0:T(8,128)(2,1)S(1)} %bitcast.20, f32[128]{0:T(128)S(1)} %mul.101, f32[128,320]{0,1:T(8,128)S(1)} %fusion.34), kind=kOutput, calls=%fused_computation.20 | convolution fusion | flops 630292480 | bytes 2785792
  130.2 0.0 reduce-scatter.9.cloned.1.call-update
  130.2 0.0 all-gather.9.cloned.1.call-start
  130.3 32.2 %reduce-scatter.7.cloned.1.call-done = f32[160,320]{1,0:T(8,128)} async-done(((f32[1280,320]{1,0:T(8,128)}), f32[160,320]{1,0:T(8,128)}) %reduce-scatter.7.cloned.1.call-update) | async-done | bytes 204816 | tf_op jit(solution)/shard_map/reduce_scatter | solution.py:44
  162.5 0.0 all-gather.9.cloned.1.call-update
  162.5 0.0 all-gather.11.cloned.1.call-start
  162.5 36.2 %reduce-scatter.9.cloned.1.call-done = f32[160,320]{1,0:T(8,128)} async-done(((f32[1280,320]{1,0:T(8,128)}), f32[160,320]{1,0:T(8,128)}) %reduce-scatter.9.cloned.1.call-update) | async-done | bytes 204816 | tf_op jit(solution)/shard_map/reduce_scatter | solution.py:45
  198.8 0.0 all-gather.11.cloned.1.call-update
  198.8 0.0 all-reduce.5.cloned.1.call-start
  199.5 0.0 copy-start.9
  199.5 27.1 %all-gather.9.cloned.1.call-done = f32[1280,320]{1,0:T(8,128)} async-done(((f32[160,320]{1,0:T(8,128)}), f32[1280,320]{1,0:T(8,128)}) %all-gather.9.cloned.1.call-update) | async-done | bytes 1638416 | tf_op jit(solution)/shard_map/all_gather | solution.py:49
  226.6 2.7 multiply_reduce_fusion.1
  229.3 26.5 %all-gather.11.cloned.1.call-done = f32[1280,320]{1,0:T(8,128)} async-done(((f32[160,320]{1,0:T(8,128)}), f32[1280,320]{1,0:T(8,128)}) %all-gather.11.cloned.1.call-update) | async-done | bytes 1638416 | tf_op jit(solution)/shard_map/all_gather | solution.py:50
  255.7 2.7 multiply_reduce_fusion
  259.7 10.5 %psum.22 = f32[]{:T(128)} all-reduce(f32[]{:T(128)S(6)} %add.42), channel_id=1, replica_groups=mesh['hid'=4,'tok'=8] {'hid'}, use_global_device_ids=true, to_apply=%region_5.6 | all-reduce | flops 1 | bytes 8 | tf_op jit(solution)/shard_map/psum | solution.py:52
  270.9 0.0 copy-done.9
  270.9 0.0 copy-start.1
  270.9 3.3 %fusion.8 = f32[64,320]{1,0:T(8,128)S(1)} fusion(bf16[64,1280]{1,0:T(8,128)(2,1)S(1)} %copy-done.9, f32[1280,320]{1,0:T(8,128)} %all-gather.9.cloned.1.call-done, f32[1280,320]{1,0:T(8,128)} %all-gather.5.cloned.1.call-done, f32[]{:T(128)S(6)} %min.3, f32[]{:T(128)} %bitcast), kind=kOutput, calls=%fused_computation.13 | convolution fusion | flops 315801600 | bytes 3522568 | tf_op jit(solution)/shard_map/dot_general | solution.py:59
  274.2 0.0 copy-done.1
  274.2 0.0 copy-start.5
  274.3 0.0 copy-start.6
  274.3 0.0 copy-start.7
  274.3 2.9 fusion
  277.2 0.0 all-reduce.5.cloned.1.call-update
  277.2 0.0 copy-done.5
  277.2 0.1 copy.18
  277.4 0.1 copy.22
  277.5 0.1 copy.27
  277.7 0.4 copy-done.8
  278.1 0.1 copy.29
  278.3 0.1 multiply_subtract_fusion
  278.4 0.8 copy.23
  279.2 0.8 copy.24
  280.0 38.5 %all-reduce.5.cloned.1.call-done = f32[64,1280]{1,0:T(8,128)} async-done(((f32[64,1280]{1,0:T(8,128)}), f32[64,1280]{1,0:T(8,128)}) %all-reduce.5.cloned.1.call-update) | async-done | bytes 327696 | tf_op jit(solution)/shard_map/psum | solution.py:60
  318.5 1.7 add_convert_fusion
  (5 shorter events, 0.0 us)
Async XLA Ops:
  7.2 33.3 %all-gather.5.cloned.1.call-start = ((), (), s32[]{:S(2)}) async-start(), calls=%async_computation.2 | async-start | bytes 2211840 | tf_op jit(solution)/shard_map/all_gather | solution.py:26
  7.9 61.7 %all-gather.7.cloned.1.call-start = ((), (), s32[]{:S(2)}) async-start(), calls=%async_computation.3 | async-start | bytes 2211840 | tf_op jit(solution)/shard_map/all_gather | solution.py:27
  8.6 108.7 %all-reduce.3.cloned.1.call-start = ((), (), s32[]{:S(2)}) async-start(), calls=%async_computation.4 | async-start | bytes 655360 | tf_op jit(solution)/shard_map/psum | solution.py:32
  43.8 30.5 %copy-start.10 = (f32[2,64]{1,0:T(2,128)S(1)}, f32[2,64]{1,0:T(2,128)}, u32[]{:S(2)}) copy-start(f32[2,64]{1,0:T(2,128)} %param.11) | copy-start | bytes 1540
  43.8 73.5 %copy-start.2 = (bf16[2,64,1280]{2,1,0:T(8,128)(2,1)S(1)}, bf16[2,64,1280]{2,1,0:T(8,128)(2,1)}, u32[]{:S(2)}) copy-start(bf16[2,64,1280]{2,1,0:T(8,128)(2,1)} %param.8) | copy-start | bytes 983044
  43.8 73.5 %copy-start.3 = (bf16[2,64,1280]{2,1,0:T(8,128)(2,1)S(1)}, bf16[2,64,1280]{2,1,0:T(8,128)(2,1)}, u32[]{:S(2)}) copy-start(bf16[2,64,1280]{2,1,0:T(8,128)(2,1)} %param.9) | copy-start | bytes 983044
  69.6 47.8 %copy-start = (f32[1280,320]{1,0:T(8,128)S(1)}, f32[1280,320]{1,0:T(8,128)}, u32[]{:S(2)}) copy-start(f32[1280,320]{1,0:T(8,128)} %all-gather.7.cloned.1.call-done) | copy-start | bytes 4915204
  74.2 88.2 %reduce-scatter.7.cloned.1.call-start = ((), (), s32[]{:S(2)}) async-start(), calls=%async_computation.8 | async-start | bytes 2211840 | tf_op jit(solution)/shard_map/reduce_scatter | solution.py:44
  123.6 2.9 copy-start.4
  126.5 72.3 %reduce-scatter.9.cloned.1.call-start = ((), (), s32[]{:S(2)}) async-start(), calls=%async_computation.9 | async-start | bytes 2211840 | tf_op jit(solution)/shard_map/reduce_scatter | solution.py:45
  130.2 96.4 %all-gather.9.cloned.1.call-start = ((), (), s32[]{:S(2)}) async-start(), calls=%async_computation.5 | async-start | bytes 2211840 | tf_op jit(solution)/shard_map/all_gather | solution.py:49
  162.5 93.3 %all-gather.11.cloned.1.call-start = ((), (), s32[]{:S(2)}) async-start(), calls=%async_computation.6 | async-start | bytes 2211840 | tf_op jit(solution)/shard_map/all_gather | solution.py:50
  198.8 119.7 %all-reduce.5.cloned.1.call-start = ((), (), s32[]{:S(2)}) async-start(), calls=%async_computation.7 | async-start | bytes 655360 | tf_op jit(solution)/shard_map/psum | solution.py:60
  199.5 71.5 %copy-start.9 = (bf16[64,1280]{1,0:T(8,128)(2,1)S(1)}, bf16[64,1280]{1,0:T(8,128)(2,1)}, u32[]{:S(2)}) copy-start(bf16[64,1280]{1,0:T(8,128)(2,1)} %param.10) | copy-start | bytes 491524
  270.9 3.3 %copy-start.1 = (f32[1280,320]{1,0:T(8,128)S(1)}, f32[1280,320]{1,0:T(8,128)}, u32[]{:S(2)}) copy-start(f32[1280,320]{1,0:T(8,128)} %all-gather.11.cloned.1.call-done) | copy-start | bytes 4915204
  274.2 2.9 copy-start.5
  274.3 3.1 copy-start.6
  274.3 3.2 copy-start.7
  277.2 0.9 copy-start.8
Sparse Core Ops, SparseCore 0:
  9.6 30.7 all-gather.4
  42.1 27.4 all-gather.6
  74.3 42.9 all-reduce.2
  126.6 35.8 reduce-scatter.6
  164.6 34.0 reduce-scatter.8
  200.2 26.3 all-gather.8
  228.2 27.4 all-gather.10
  277.3 41.1 all-reduce.4
where the time goes:
time: 327 us
  waiting for transfers between devices  260 us (80%)
  matrix products  24 us (7%)
  between operations  18.3 us (6%)
  blocking collectives  10.5 us (3%)
  other arithmetic  7.21 us (2%)
  local copies, waits for them, and re-layouts  6.97 us (2%)
    psum x1, waiting for transfers between devices, on_device(): lax.psum(times_transposed(hidden, full_read).astype(jnp.bfloat16), 'hid')  42.8 us
    psum x1, waiting for transfers between devices, on_device(): answer = lax.psum(times_transposed(query_hidden, wide_read), 'hid')  38.5 us
    reduce_scatter x1, waiting for transfers between devices, on_device(): lax.psum_scatter(grad_read, 'tok', scatter_dimension=0, tiled=True)  36.2 us
    reduce_scatter x1, waiting for transfers between devices, on_device(): lax.psum_scatter(grad_write, 'tok', scatter_dimension=0, tiled=True)  32.2 us
    all_gather x1, waiting for transfers between devices, on_device(): lax.all_gather(write_weight, 'tok', axis=0, tiled=True)  29.1 us
    all_gather x1, waiting for transfers between devices, on_device(): lax.all_gather(part_w, 'tok', axis=0, tiled=True)  27.1 us
    all_gather x1, waiting for transfers between devices, on_device(): lax.all_gather(part_r, 'tok', axis=0, tiled=True)  26.5 us
    all_gather x1, waiting for transfers between devices, on_device(): lax.all_gather(read_weight, 'tok', axis=0, tiled=True)  25.7 us
  transfers between devices with their start and end apart: 8, of which 8 were waited for; matrix products, arithmetic and copies ran while one was open for 4% of the time, Pallas kernels for 0%

commit v1 on v0

--- a/solution.py
+++ b/solution.py
@@ -5,6 +5,16 @@
 
 highest = lax.Precision.HIGHEST
 radius = 12.0
+
+
+def render_corner(vector):
+    sheets = []
+    for _ in range(lax.axis_size("tok")):
+        sheets.append(vector)
+    s_next = jnp.stack(sheets, 0)
+    return jnp.concatenate(
+        lax.all_to_all(s_next, axis_name="tok", split_axis=0, concat_axis=0), axis=0
+    )
 
 
 def silu_slope(z):
@@ -45,10 +55,7 @@
         lax.psum_scatter(grad_read, "tok", scatter_dimension=0, tiled=True),
     )
     keep = (1.0 - forget[0]) * (1.0 - forget[1])
-    whole_w, whole_r = (
-        lax.all_gather(part_w, "tok", axis=0, tiled=True),
-        lax.all_gather(part_r, "tok", axis=0, tiled=True),
-    )
+    whole_w, whole_r = (lax.all_gather(part_w, "tok", axis=0, tiled=True), render_corner(part_r))
     total = lax.psum(jnp.sum(whole_w * whole_w) + jnp.sum(whole_r * whole_r), "hid")
     scale = jnp.minimum(1.0, radius / jnp.sqrt(total + 1e-06))
     new_write = keep * write_weight - scale * part_w

time: 327 us -> 340 us (1.040)
  waiting for transfers between devices: 260 us -> 265 us
  starting transfers between devices: 0.32 us -> 4.6 us
  local copies, waits for them, and re-layouts: 6.97 us -> 10.7 us
    all_gather x1 -> x0, waiting for transfers between devices: 26.5 us -> none  [on_device(): lax.all_gather(part_r, 'tok', axis=0, tiled=True)]
    all_to_all x0 -> x1, waiting for transfers between devices: none -> 21.8 us  [render_corner(): lax.all_to_all(s_next, axis_name='tok', split_axis=0, concat_axis=0)]
    all_gather x1, waiting for transfers between devices: 27.1 us -> 36.8 us  [on_device(): lax.all_gather(part_w, 'tok', axis=0, tiled=True)]
    all_to_all x0 -> x1, starting transfers between devices: none -> 4.32 us  [render_corner(): lax.all_to_all(s_next, axis_name='tok', split_axis=0, concat_axis=0)]
    unnamed x29 -> x31, local copies, waits for them, and re-layouts: 5.57 us -> 7 us
  transfers between devices with their start and end apart: 8 -> 8, of which waited for: 8 -> 8; matrix products, arithmetic and copies ran while one was open for 4% -> 5% of each run, Pallas kernels for 0% -> 0%
where the time goes in v1:
time: 340 us
  waiting for transfers between devices  265 us (78%)
  matrix products  21.7 us (6%)
  between operations  18.3 us (5%)
  local copies, waits for them, and re-layouts  10.7 us (3%)
  blocking collectives  10.6 us (3%)
  other arithmetic  9.15 us (3%)
  starting transfers between devices  4.6 us (1%)
    psum x1, waiting for transfers between devices, on_device(): lax.psum(times_transposed(hidden, full_read).astype(jnp.bfloat16), 'hid')  42.8 us
    psum x1, waiting for transfers between devices, on_device(): answer = lax.psum(times_transposed(query_hidden, wide_read), 'hid')  38.3 us
    all_gather x1, waiting for transfers between devices, on_device(): lax.all_gather(part_w, 'tok', axis=0, tiled=True)  36.8 us
    reduce_scatter x1, waiting for transfers between devices, on_device(): lax.psum_scatter(grad_read, 'tok', scatter_dimension=0, tiled=True)  36.3 us
    reduce_scatter x1, waiting for transfers between devices, on_device(): lax.psum_scatter(grad_write, 'tok', scatter_dimension=0, tiled=True)  32.2 us
    all_gather x1, waiting for transfers between devices, on_device(): lax.all_gather(write_weight, 'tok', axis=0, tiled=True)  29.1 us
    all_gather x1, waiting for transfers between devices, on_device(): lax.all_gather(read_weight, 'tok', axis=0, tiled=True)  25.7 us
    all_to_all x1, waiting for transfers between devices, render_corner(): lax.all_to_all(s_next, axis_name='tok', split_axis=0, concat_axis=0)  21.8 us
  transfers between devices with their start and end apart: 8, of which 8 were waited for; matrix products, arithmetic and copies ran while one was open for 5% of the time, Pallas kernels for 0%

profile of v1, /device:TPU:0, one launch (start us, length us, event | category | flops | bytes accessed | tf_op | source)
XLA Modules:
  0.0 339.7 jit_solution(4556793764941514454)
XLA Ops:
  7.2 0.0 all-gather.4.cloned.1.call-start
  7.2 0.7 all-gather.4.cloned.1.call-update
  7.9 0.0 all-gather.6.cloned.1.call-start
  7.9 0.7 all-gather.6.cloned.1.call-update
  8.6 0.0 all-reduce.3.cloned.1.call-start
  9.3 1.3 fusion.28
  11.3 29.1 %all-gather.4.cloned.1.call-done = f32[1280,320]{1,0:T(8,128)} async-done(((f32[160,320]{1,0:T(8,128)}), f32[1280,320]{1,0:T(8,128)}) %all-gather.4.cloned.1.call-update) | async-done | bytes 1638416 | tf_op jit(solution)/shard_map/all_gather | solution.py:36
  40.4 3.4 fusion.29
  43.8 0.0 copy-start.11
  43.8 0.0 copy-start.3
  43.8 0.0 copy-start.4
  43.8 25.7 %all-gather.6.cloned.1.call-done = f32[1280,320]{1,0:T(8,128)} async-done(((f32[160,320]{1,0:T(8,128)}), f32[1280,320]{1,0:T(8,128)}) %all-gather.6.cloned.1.call-update) | async-done | bytes 1638416 | tf_op jit(solution)/shard_map/all_gather | solution.py:37
  69.6 4.6 %convolution_convert_fusion = bf16[128,1280]{1,0:T(8,128)(2,1)} fusion(f32[1280,320]{1,0:T(8,128)} %all-gather.6.cloned.1.call-done, f32[128,320]{0,1:T(8,128)S(1)} %fusion.29), kind=kOutput, calls=%fused_computation.1 | convolution fusion | flops 629473280 | bytes 2129920 | tf_op jit(solution)/shard_map/dot_general | solution.py:26
  74.2 0.0 all-reduce.3.cloned.1.call-update
  74.2 0.0 reduce-scatter.7.cloned.1.call-start
  74.3 0.1 maximum_multiply_fusion
  74.3 0.0 copy-done.11
  74.3 0.1 broadcast_multiply_fusion.1
  74.4 0.1 mul.107
  74.5 42.8 %all-reduce.3.cloned.1.call-done = bf16[128,1280]{1,0:T(8,128)(2,1)} async-done(((bf16[128,1280]{1,0:T(8,128)(2,1)}), bf16[128,1280]{1,0:T(8,128)(2,1)}) %all-reduce.3.cloned.1.call-update) | async-done | bytes 327696 | tf_op jit(solution)/shard_map/psum | solution.py:42
  117.3 0.0 copy-done.3
  117.4 0.0 copy-done.4
  117.4 0.0 copy-done
  117.4 4.3 %convolution_multiply_fusion = f32[128,320]{0,1:T(8,128)S(1)} fusion(f32[1280,320]{1,0:T(8,128)S(1)} %copy-done, bf16[128,1280]{1,0:T(8,128)(2,1)S(1)} %bitcast.24, bf16[128,1280]{1,0:T(8,128)(2,1)} %all-reduce.3.cloned.1.call-done, bf16[128,1280]{1,0:T(8,128)(2,1)S(1)} %bitcast.21, f32[128]{0:T(128)S(1)} %mul.107, f32[128,320]{0,1:T(8,128)S(1)} %fusion.29), kind=kOutput, calls=%fused_computation.9 | convolution fusion | flops 630456320 | bytes 2949632 | tf_op jit(solution)/shard_map/dot_general | solution.py:50
  121.6 2.0 convolution_bitcast_fusion
  123.6 2.8 copy.35
  126.4 0.0 reduce-scatter.7.cloned.1.call-update
  126.5 0.0 reduce-scatter.9.cloned.1.call-start
  126.5 0.0 copy-done.5
  126.5 3.7 %fusion.10 = f32[1280,320]{1,0:T(8,128)} fusion(bf16[128,1280]{1,0:T(8,128)(2,1)S(1)} %bitcast.25, bf16[128,1280]{1,0:T(8,128)(2,1)S(1)} %copy-done.5, bf16[128,1280]{1,0:T(8,128)(2,1)S(1)} %bitcast.23, f32[128]{0:T(128)S(1)} %mul.107, f32[128,320]{0,1:T(8,128)S(1)} %fusion.29), kind=kOutput, calls=%fused_computation.16 | convolution fusion | flops 630292480 | bytes 2785792
  130.2 0.0 reduce-scatter.9.cloned.1.call-update
  130.2 0.0 all-gather.8.cloned.1.call-start
  130.3 32.2 %reduce-scatter.7.cloned.1.call-done = f32[160,320]{1,0:T(8,128)} async-done(((f32[1280,320]{1,0:T(8,128)}), f32[160,320]{1,0:T(8,128)}) %reduce-scatter.7.cloned.1.call-update) | async-done | bytes 204816 | tf_op jit(solution)/shard_map/reduce_scatter | solution.py:54
  162.5 0.0 all-gather.8.cloned.1.call-update
  162.5 36.3 %reduce-scatter.9.cloned.1.call-done = f32[160,320]{1,0:T(8,128)} async-done(((f32[1280,320]{1,0:T(8,128)}), f32[160,320]{1,0:T(8,128)}) %reduce-scatter.9.cloned.1.call-update) | async-done | bytes 204816 | tf_op jit(solution)/shard_map/reduce_scatter | solution.py:55
  198.8 2.3 stack.5
  201.1 4.3 %all-to-all-start = ((f32[8,160,320]{2,1,0:T(8,128)}), f32[8,160,320]{2,1,0:T(8,128)}, u32[]{:S(2)}, u32[]{:S(2)}) async-start(f32[8,160,320]{2,1,0:T(8,128)} %stack.5), calls=%async_computation | async-start | bytes 3932160 | tf_op jit(solution)/shard_map/all_to_all | solution.py:16
  205.4 0.0 all-reduce.5.cloned.1.call-start
  206.1 36.8 %all-gather.8.cloned.1.call-done = f32[1280,320]{1,0:T(8,128)} async-done(((f32[160,320]{1,0:T(8,128)}), f32[1280,320]{1,0:T(8,128)}) %all-gather.8.cloned.1.call-update) | async-done | bytes 1638416 | tf_op jit(solution)/shard_map/all_gather | solution.py:58
  243.0 2.7 multiply_reduce_fusion.1
  245.6 21.8 %all-to-all-done = f32[8,160,320]{2,1,0:T(8,128)} async-done(((f32[8,160,320]{2,1,0:T(8,128)}), f32[8,160,320]{2,1,0:T(8,128)}, u32[]{:S(2)}, u32[]{:S(2)}) %all-to-all-start) | async-done | bytes 1638432 | tf_op jit(solution)/shard_map/all_to_all | solution.py:16
  267.5 2.7 multiply_reduce_fusion
  271.4 10.6 %psum.22 = f32[]{:T(128)} all-reduce(f32[]{:T(128)S(6)} %add.42), channel_id=1, replica_groups=mesh['hid'=4,'tok'=8] {'hid'}, use_global_device_ids=true, to_apply=%region_5.6 | all-reduce | flops 1 | bytes 8 | tf_op jit(solution)/shard_map/psum | solution.py:59
  282.7 1.7 broadcast_multiply_fusion
  284.4 0.0 copy-start.10
  284.4 0.3 bitcast_subtract_fusion
  284.6 1.3 copy-done.1
  285.9 0.6 copy-done.2
  286.5 1.0 fusion.4
  287.5 0.0 copy-start.6
  287.5 0.0 copy-start.7
  287.6 2.8 fusion.16
  290.4 0.0 all-reduce.5.cloned.1.call-update
  290.4 0.1 copy.27
  290.6 0.1 copy.31
  290.7 0.0 copy-done.8
  290.7 0.1 copy.36
  290.9 0.0 copy-done.9
  290.9 0.1 copy.38
  291.0 0.1 multiply_subtract_fusion
  291.1 0.8 copy.32
  292.0 0.8 copy.33
  292.8 38.3 %all-reduce.5.cloned.1.call-done = f32[64,1280]{1,0:T(8,128)} async-done(((f32[64,1280]{1,0:T(8,128)}), f32[64,1280]{1,0:T(8,128)}) %all-reduce.5.cloned.1.call-update) | async-done | bytes 327696 | tf_op jit(solution)/shard_map/psum | solution.py:67
  331.1 1.7 add_convert_fusion
  (9 shorter events, 0.0 us)
Async XLA Ops:
  7.2 33.3 %all-gather.4.cloned.1.call-start = ((), (), s32[]{:S(2)}) async-start(), calls=%async_computation.3 | async-start | bytes 2211840 | tf_op jit(solution)/shard_map/all_gather | solution.py:36
  7.9 61.7 %all-gather.6.cloned.1.call-start = ((), (), s32[]{:S(2)}) async-start(), calls=%async_computation.4 | async-start | bytes 2211840 | tf_op jit(solution)/shard_map/all_gather | solution.py:37
  8.6 108.7 %all-reduce.3.cloned.1.call-start = ((), (), s32[]{:S(2)}) async-start(), calls=%async_computation.5 | async-start | bytes 655360 | tf_op jit(solution)/shard_map/psum | solution.py:42
  43.8 30.5 %copy-start.11 = (f32[2,64]{1,0:T(2,128)S(1)}, f32[2,64]{1,0:T(2,128)}, u32[]{:S(2)}) copy-start(f32[2,64]{1,0:T(2,128)} %param.11) | copy-start | bytes 1540
  43.8 73.5 %copy-start.3 = (bf16[2,64,1280]{2,1,0:T(8,128)(2,1)S(1)}, bf16[2,64,1280]{2,1,0:T(8,128)(2,1)}, u32[]{:S(2)}) copy-start(bf16[2,64,1280]{2,1,0:T(8,128)(2,1)} %param.8) | copy-start | bytes 983044
  43.8 73.5 %copy-start.4 = (bf16[2,64,1280]{2,1,0:T(8,128)(2,1)S(1)}, bf16[2,64,1280]{2,1,0:T(8,128)(2,1)}, u32[]{:S(2)}) copy-start(bf16[2,64,1280]{2,1,0:T(8,128)(2,1)} %param.9) | copy-start | bytes 983044
  69.6 47.8 %copy-start = (f32[1280,320]{1,0:T(8,128)S(1)}, f32[1280,320]{1,0:T(8,128)}, u32[]{:S(2)}) copy-start(f32[1280,320]{1,0:T(8,128)} %all-gather.6.cloned.1.call-done) | copy-start | bytes 4915204
  74.2 88.2 %reduce-scatter.7.cloned.1.call-start = ((), (), s32[]{:S(2)}) async-start(), calls=%async_computation.8 | async-start | bytes 2211840 | tf_op jit(solution)/shard_map/reduce_scatter | solution.py:54
  123.6 2.9 copy-start.5
  126.5 72.3 %reduce-scatter.9.cloned.1.call-start = ((), (), s32[]{:S(2)}) async-start(), calls=%async_computation.9 | async-start | bytes 2211840 | tf_op jit(solution)/shard_map/reduce_scatter | solution.py:55
  130.2 112.7 %all-gather.8.cloned.1.call-start = ((), (), s32[]{:S(2)}) async-start(), calls=%async_computation.6 | async-start | bytes 2211840 | tf_op jit(solution)/shard_map/all_gather | solution.py:58
  201.1 66.4 %all-to-all-start = ((f32[8,160,320]{2,1,0:T(8,128)}), f32[8,160,320]{2,1,0:T(8,128)}, u32[]{:S(2)}, u32[]{:S(2)}) async-start(f32[8,160,320]{2,1,0:T(8,128)} %stack.5), calls=%async_computation | async-start | bytes 3932160 | tf_op jit(solution)/shard_map/all_to_all | solution.py:16
  205.4 125.7 %all-reduce.5.cloned.1.call-start = ((), (), s32[]{:S(2)}) async-start(), calls=%async_computation.7 | async-start | bytes 655360 | tf_op jit(solution)/shard_map/psum | solution.py:67
  284.4 1.5 copy-start.1
  284.4 2.1 copy-start.2
  284.4 2.1 copy-start.10
  287.5 2.9 copy-start.6
  287.5 3.0 copy-start.7
  287.6 3.2 copy-start.8
  287.6 3.3 copy-start.9
Sparse Core Ops, SparseCore 0:
  9.6 30.7 all-gather.3
  42.1 27.4 all-gather.5
  74.3 42.9 all-reduce.2
  126.6 35.8 reduce-scatter.6
  164.6 34.0 reduce-scatter.8
  200.2 42.6 all-gather.7
  290.5 40.5 all-reduce.4
